TPU v7x, 256 devices: a 8x8x2 block of a 8x8x16 slice. The times are simulated.
256 devices in a mesh: groups: 2 (over z), dp: 64 (over y, x), mp: 2 (over core).
Axes of the slice: x: 8, y: 8, z: 2, core: 2. Of those that a mesh axis runs over, the one named last changes fastest.
The devices are a block of a 8x8x16 slice.
Arguments:
- tokens: bfloat16 [32768, 8192], P(('groups', 'dp'), 'mp'), parts along dimension 0, may hold values from -6 to 6
- queries: bfloat16 [32768, 8192], P(('groups', 'dp'), 'mp'), parts along dimension 0, may hold values from -384 to 384, as said below
- w_key: bfloat16 [8192, 1024], P('dp', 'mp'), may hold values from -0.0625 to 0.0625
- w_value: bfloat16 [8192, 1024], P('dp', 'mp'), may hold values from -0.0625 to 0.0625
- lengths: int32 [16, 16], P('groups'), parts along dimension 0, may hold values from 1 to 1920, 2048 in all within a row
Outputs:
- attended: bfloat16 [32768, 8192], P(('groups', 'dp'), 'mp'), parts along dimension 0
There are 2 independent parts, one for each index of `groups`. A program takes and returns all parts, laid end to end along the dimension named above; an argument that names none is the same for every part. Nothing has to cross between parts.
Inputs may be any that keep to these rules, and one draw needn't show every extreme that they name: Real-valued queries.
All inputs are finite; a program needn't handle non-finite values.
Results may differ from a plain program's by a relative error of at most 0.0055.
The roundings to bfloat16 on the way count: a program that leaves them out, or rounds other values in their place, can miss the bound.
Values may be sent and summed in bfloat16 or wider, within the bound.
A program may use at most 128 MiB of HBM per device.

v0:
```python
import math

import jax
import jax.numpy as jnp
from jax import lax
from jax.sharding import PartitionSpec as P

DH = 128
ROW = 2048


def side_by_side(arrays, axis, dim, along):
    widths = [a.shape[along] for a in arrays]
    both = jnp.concatenate(arrays, axis=along)
    result = lax.all_gather(both, axis, axis=dim, tiled=True)
    return tuple(jnp.split(result, [sum(widths[:k]) for k in range(1, len(widths))], axis=along))


def shifted(block, axis, distance):
    devices = range(lax.axis_size(axis))
    route = [((i - distance) % len(devices), i) for i in devices]
    return lax.ppermute(block, axis, route)


def rotate(values, positions):
    half_dim = values.shape[-1] // 2
    frequency = jnp.power(
        500000.0, -2.0 * jnp.arange(half_dim, dtype=jnp.float32) / values.shape[-1]
    )
    angles = positions.astype(jnp.float32)[:, None] * frequency[None, :]
    cosine = jnp.cos(angles)[:, None, :]
    sine_part = jnp.sin(angles)[:, None, :]
    first_half = values[..., :half_dim]
    second_half = values[..., half_dim:]
    return jnp.concatenate(
        [
            first_half * cosine - second_half * sine_part,
            second_half * cosine + first_half * sine_part,
        ],
        axis=-1,
    )


def per_device(tokens, queries, w_key, w_value, lengths):
    tok_count = tokens.shape[0]
    head_dim = DH
    full_tokens = lax.all_gather(tokens, "mp", axis=1, tiled=True)
    kv_local = w_key.shape[1] // head_dim
    group_size = queries.shape[1] // head_dim // kv_local

    def add_rows(weight_rows):
        return jnp.dot(full_tokens, weight_rows, preferred_element_type=jnp.float32)

    weight_pair = side_by_side((w_key, w_value), "dp", 0, 1)
    key_sum = add_rows(weight_pair[0])
    value_sum = add_rows(weight_pair[1])
    all_tokens = tok_count * lax.axis_size("dp")
    first_token = (lax.axis_index("dp") * tok_count - ROW // 2 + all_tokens) % all_tokens
    row_index = first_token // ROW
    row_lengths = lax.dynamic_slice_in_dim(lengths, row_index, 1, 0)[0]
    finish = jnp.cumsum(row_lengths)

    def locate(offsets):
        before = finish[None, :] <= offsets[:, None]
        sequence = jnp.sum(before.astype(jnp.int32), axis=1)
        started = jnp.sum(jnp.where(before, row_lengths[None, :], 0), axis=1)
        return (sequence, offsets - started)

    own_offsets = first_token - row_index * ROW + jnp.arange(tok_count, dtype=jnp.int32)
    own_sequence, own_positions = locate(own_offsets)
    rotated = rotate(key_sum.reshape(tok_count, kv_local, head_dim), own_positions)
    local_keys = rotated.reshape(tok_count, kv_local * head_dim).astype(jnp.bfloat16)
    local_values = value_sum.astype(jnp.bfloat16)
    stacked = jnp.stack([local_keys, local_values])
    row_devices = ROW // tok_count
    pieces = [stacked]
    passed = stacked
    for distance in range(1, row_devices):
        passed = shifted(passed, "dp", 1)
        pieces.insert(0, passed)
    window = jnp.concatenate(pieces, axis=1)
    window_offsets = (
        own_offsets[0]
        - (row_devices - 1) * tok_count
        + jnp.arange(row_devices * tok_count, dtype=jnp.int32)
    )
    inside = window_offsets >= 0
    window_sequence, unused = locate(jnp.maximum(window_offsets, 0))
    allowed = (
        inside[None, :]
        & (window_sequence[None, :] == own_sequence[:, None])
        & (window_offsets[None, :] <= own_offsets[:, None])
    )
    scale_factor = 1.0 / math.sqrt(head_dim)
    outputs = []
    for kv_head in range(kv_local):
        query_part = queries[
            :, kv_head * group_size * head_dim : (kv_head + 1) * group_size * head_dim
        ].reshape(tok_count, group_size, head_dim)
        key_part = window[0, :, kv_head * head_dim : (kv_head + 1) * head_dim]
        value_part = window[1, :, kv_head * head_dim : (kv_head + 1) * head_dim]
        scores = (
            jnp.einsum("tgd,wd->gtw", query_part, key_part, preferred_element_type=jnp.float32)
            * scale_factor
        )
        masked = jnp.where(allowed[None], scores, -1e30)
        row_peak = jnp.max(masked, axis=-1, keepdims=True)
        weights = jnp.where(allowed[None], jnp.exp(masked - row_peak), 0.0)
        probability = (weights / jnp.sum(weights, axis=-1, keepdims=True)).astype(jnp.bfloat16)
        mixed_heads = jnp.einsum(
            "gtw,wd->tgd", probability, value_part, preferred_element_type=jnp.float32
        )
        outputs.append(mixed_heads.reshape(tok_count, group_size * head_dim).astype(jnp.bfloat16))
    return jnp.concatenate(outputs, axis=1)


def solution(mesh):
    return jax.shard_map(
        per_device,
        mesh=mesh,
        in_specs=(
            P(("groups", "dp"), "mp"),
            P(("groups", "dp"), "mp"),
            P("dp", "mp"),
            P("dp", "mp"),
            P("groups", None),
        ),
        out_specs=P(("groups", "dp"), "mp"),
        check_vma=False,
    )
```

profile of v0, /device:TPU:514, one launch (start us, length us, event | category | flops | bytes accessed | tf_op | source)
XLA Modules:
  0.0 389.3 jit_solution(7679930989265311872)
XLA Ops:
  7.4 1.7 pad_maximum_fusion.2
  10.5 36.9 %all-gather.5.cloned.1.call-done = bf16[256,8192]{1,0:T(8,128)(2,1)} async-done(((bf16[256,4096]{1,0:T(8,128)(2,1)}), bf16[256,8192]{1,0:T(8,128)(2,1)}) %all-gather.5.cloned.1.call-update) | async-done | bytes 4194320 | tf_op jit(solution)/shard_map/all_gather | solution.py:47
  47.5 140.2 %all-gather.3.cloned.1.call-done = bf16[8192,1024]{1,0:T(8,128)(2,1)} async-done(((bf16[128,1024]{1,0:T(8,128)(2,1)}), bf16[8192,1024]{1,0:T(8,128)(2,1)}) %all-gather.3.cloned.1.call-update) | async-done | bytes 16777232 | tf_op jit(solution)/shard_map/all_gather | solution.py:15
  187.7 7.1 %fusion.10 = f32[512,256]{1,0:T(8,128)S(1)} fusion(bf16[256,8192]{1,0:T(8,128)(2,1)} %all-gather.5.cloned.1.call-done, bf16[8192,1024]{1,0:T(8,128)(2,1)} %all-gather.3.cloned.1.call-done), kind=kOutput, calls=%fused_computation.22 | convolution fusion | flops 2147483648 | bytes 13107200 | tf_op jit(solution)/shard_map/dot_general | solution.py:52
  195.0 7.1 %fusion.43 = bf16[1,256,512]{2,1,0:T(8,128)(2,1)S(1)} fusion(bf16[256,8192]{1,0:T(8,128)(2,1)} %all-gather.5.cloned.1.call-done, bf16[8192,1024]{1,0:T(8,128)(2,1)} %all-gather.3.cloned.1.call-done), kind=kOutput, calls=%fused_computation.51 | convolution fusion | flops 2147614720 | bytes 12845056 | tf_op jit(solution)/shard_map/dot_general | solution.py:52
  202.2 1.6 collective-permute-start
  203.8 12.0 %collective-permute-done = bf16[2,256,512]{2,1,0:T(8,128)(2,1)S(1)} collective-permute-done((bf16[2,256,512]{2,1,0:T(8,128)(2,1)S(1)}, bf16[2,256,512]{2,1,0:T(8,128)(2,1)S(1)}, u32[]{:S(2)}, u32[]{:S(2)}) %collective-permute-start) | collective-permute-done | bytes 524320 | tf_op jit(solution)/shard_map/ppermute | solution.py:22
  217.3 13.3 %collective-permute-done.1 = bf16[2,256,512]{2,1,0:T(8,128)(2,1)S(1)} collective-permute-done((bf16[2,256,512]{2,1,0:T(8,128)(2,1)S(1)}, bf16[2,256,512]{2,1,0:T(8,128)(2,1)S(1)}, u32[]{:S(2)}, u32[]{:S(2)}) %collective-permute-start.1) | collective-permute-done | bytes 524320 | tf_op jit(solution)/shard_map/ppermute | solution.py:22
  230.6 15.1 %collective-permute-done.2 = bf16[2,256,512]{2,1,0:T(8,128)(2,1)S(1)} collective-permute-done((bf16[2,256,512]{2,1,0:T(8,128)(2,1)S(1)}, bf16[2,256,512]{2,1,0:T(8,128)(2,1)S(1)}, u32[]{:S(2)}, u32[]{:S(2)}) %collective-permute-start.2) | collective-permute-done | bytes 524320 | tf_op jit(solution)/shard_map/ppermute | solution.py:22
  246.5 14.2 %collective-permute-done.3 = bf16[2,256,512]{2,1,0:T(8,128)(2,1)S(1)} collective-permute-done((bf16[2,256,512]{2,1,0:T(8,128)(2,1)S(1)}, bf16[2,256,512]{2,1,0:T(8,128)(2,1)S(1)}, u32[]{:S(2)}, u32[]{:S(2)}) %collective-permute-start.3) | collective-permute-done | bytes 524320 | tf_op jit(solution)/shard_map/ppermute | solution.py:22
  261.3 12.9 %collective-permute-done.4 = bf16[2,256,512]{2,1,0:T(8,128)(2,1)} collective-permute-done((bf16[2,256,512]{2,1,0:T(8,128)(2,1)S(1)}, bf16[2,256,512]{2,1,0:T(8,128)(2,1)}, u32[]{:S(2)}, u32[]{:S(2)}) %collective-permute-start.4) | collective-permute-done | bytes 524320 | tf_op jit(solution)/shard_map/ppermute | solution.py:22
  277.7 9.4 %collective-permute-done.5 = bf16[2,256,512]{2,1,0:T(8,128)(2,1)} collective-permute-done((bf16[2,256,512]{2,1,0:T(8,128)(2,1)}, bf16[2,256,512]{2,1,0:T(8,128)(2,1)}, u32[]{:S(2)}, u32[]{:S(2)}) %collective-permute-start.5) | collective-permute-done | bytes 524320 | tf_op jit(solution)/shard_map/ppermute | solution.py:22
  287.1 1.8 compare_and_fusion
  288.9 10.7 %collective-permute-done.6 = bf16[2,256,512]{2,1,0:T(8,128)(2,1)S(1)} collective-permute-done((bf16[2,256,512]{2,1,0:T(8,128)(2,1)}, bf16[2,256,512]{2,1,0:T(8,128)(2,1)S(1)}, u32[]{:S(2)}, u32[]{:S(2)}) %collective-permute-start.6) | collective-permute-done | bytes 524320 | tf_op jit(solution)/shard_map/ppermute | solution.py:22
  304.1 1.9 copy-done.7
  306.0 11.2 %fusion.65 = (f32[8,256]{1,0:T(8,128)S(1)}, f32[8,256,2048]{1,2,0:T(8,128)}) fusion(pred[256,2048]{0,1:T(8,128)(4,1)S(1)} %compare_and_fusion, bf16[256,8,128]{0,2,1:T(8,128)(2,1)S(1)} %bitcast.160, bf16[2,2048,512]{2,1,0:T(8,128)(2,1)} %copy-done.7), kind=kOutput, calls=%fused_computation.102 | convolution fusion | flops 1094715392 | bytes 18882560 | tf_op jit(solution)/shard_map/sub | solution.py:108
  317.2 7.3 %fusion.28 = bf16[128,8,256]{2,0,1:T(8,128)(2,1)S(1)} fusion(f32[8,256,2048]{1,2,0:T(8,128)} %get-tuple-element.18, f32[8,256]{1,0:T(8,128)S(1)} %get-tuple-element.17, bf16[2,2048,512]{2,1,0:T(8,128)(2,1)} %copy-done.7), kind=kOutput, calls=%fused_computation.42 | convolution fusion | flops 1082392576 | bytes 17833984 | tf_op jit(solution)/shard_map/gtw,wd->tgd/dot_general | solution.py:110
  324.7 11.2 %fusion.66 = (f32[8,256]{1,0:T(8,128)S(1)}, f32[8,256,2048]{1,2,0:T(8,128)}) fusion(pred[256,2048]{0,1:T(8,128)(4,1)S(1)} %compare_and_fusion, bf16[256,8,128]{0,2,1:T(8,128)(2,1)S(1)} %bitcast.159, bf16[2,2048,512]{2,1,0:T(8,128)(2,1)} %copy-done.7), kind=kOutput, calls=%fused_computation.103 | convolution fusion | flops 1094715392 | bytes 18882560 | tf_op jit(solution)/shard_map/sub | solution.py:108
  335.9 7.3 %fusion.29 = bf16[128,8,256]{2,0,1:T(8,128)(2,1)S(1)} fusion(f32[8,256,2048]{1,2,0:T(8,128)} %get-tuple-element.20, f32[8,256]{1,0:T(8,128)S(1)} %get-tuple-element.19, bf16[2,2048,512]{2,1,0:T(8,128)(2,1)} %copy-done.7), kind=kOutput, calls=%fused_computation.43 | convolution fusion | flops 1082392576 | bytes 17833984 | tf_op jit(solution)/shard_map/gtw,wd->tgd/dot_general | solution.py:110
  343.3 11.4 %fusion.67 = (f32[8,256]{1,0:T(8,128)S(1)}, f32[8,256,2048]{1,2,0:T(8,128)}) fusion(pred[256,2048]{0,1:T(8,128)(4,1)S(1)} %compare_and_fusion, bf16[256,8,128]{0,2,1:T(8,128)(2,1)S(1)} %bitcast.158, bf16[2,2048,512]{2,1,0:T(8,128)(2,1)} %copy-done.7), kind=kOutput, calls=%fused_computation.104 | convolution fusion | flops 1094715392 | bytes 18882560 | tf_op jit(solution)/shard_map/sub | solution.py:108
  354.8 7.3 %fusion.30 = bf16[128,8,256]{2,0,1:T(8,128)(2,1)S(1)} fusion(f32[8,256,2048]{1,2,0:T(8,128)} %get-tuple-element.22, f32[8,256]{1,0:T(8,128)S(1)} %get-tuple-element.21, bf16[2,2048,512]{2,1,0:T(8,128)(2,1)} %copy-done.7), kind=kOutput, calls=%fused_computation.44 | convolution fusion | flops 1082392576 | bytes 17833984 | tf_op jit(solution)/shard_map/gtw,wd->tgd/dot_general | solution.py:110
  362.3 11.2 %fusion.68 = (f32[8,256]{1,0:T(8,128)S(1)}, f32[8,256,2048]{1,2,0:T(8,128)}) fusion(pred[256,2048]{0,1:T(8,128)(4,1)S(1)} %compare_and_fusion, bf16[256,8,128]{0,2,1:T(8,128)(2,1)S(1)} %bitcast.157, bf16[2,2048,512]{2,1,0:T(8,128)(2,1)} %copy-done.7), kind=kOutput, calls=%fused_computation.105 | convolution fusion | flops 1094715392 | bytes 18882560 | tf_op jit(solution)/shard_map/sub | solution.py:108
  373.5 7.3 %fusion.31 = bf16[128,8,256]{2,0,1:T(8,128)(2,1)S(1)} fusion(f32[8,256,2048]{1,2,0:T(8,128)} %get-tuple-element.24, f32[8,256]{1,0:T(8,128)S(1)} %get-tuple-element.23, bf16[2,2048,512]{2,1,0:T(8,128)(2,1)} %copy-done.7), kind=kOutput, calls=%fused_computation.45 | convolution fusion | flops 1082392576 | bytes 17833984 | tf_op jit(solution)/shard_map/gtw,wd->tgd/dot_general | solution.py:110
  380.9 1.5 pad_maximum_fusion
  (60 shorter events, 13.4 us)
Async XLA Ops:
  6.5 40.9 %all-gather.5.cloned.1.call-start = ((), (), s32[]{:S(2)}) async-start(), calls=%async_computation.1 | async-start | bytes 6291456 | tf_op jit(solution)/shard_map/all_gather | solution.py:47
  7.3 180.4 %all-gather.3.cloned.1.call-start = ((), (), s32[]{:S(2)}) async-start(), calls=%async_computation | async-start | bytes 17039360 | tf_op jit(solution)/shard_map/all_gather | solution.py:15
  195.0 79.3 %copy-start = (bf16[256,4096]{1,0:T(8,128)(2,1)S(1)}, bf16[256,4096]{1,0:T(8,128)(2,1)}, u32[]{:S(2)}) copy-start(bf16[256,4096]{1,0:T(8,128)(2,1)} %param.6) | copy-start | bytes 6291460
  202.2 13.6 %collective-permute-start = (bf16[2,256,512]{2,1,0:T(8,128)(2,1)S(1)}, bf16[2,256,512]{2,1,0:T(8,128)(2,1)S(1)}, u32[]{:S(2)}, u32[]{:S(2)}) collective-permute-start(bf16[2,256,512]{2,1,0:T(8,128)(2,1)S(1)} %pad_maximum_fusion.1), channel_id=1, source_target_pairs={{126,0},{0,2},{2,4},{4,6},{6,8},{8,10},{10,12},{12,14},{14,16},{16... | collective-permute-start | bytes 1572872 | tf_op jit(solution)/shard_map/ppermute | solution.py:22
  215.8 14.8 %collective-permute-start.1 = (bf16[2,256,512]{2,1,0:T(8,128)(2,1)S(1)}, bf16[2,256,512]{2,1,0:T(8,128)(2,1)S(1)}, u32[]{:S(2)}, u32[]{:S(2)}) collective-permute-start(bf16[2,256,512]{2,1,0:T(8,128)(2,1)S(1)} %collective-permute-done), channel_id=1, source_target_pairs={{126,0},{0,2},{2,4},{4,6},{6,8},{8,10},{10,12},{12,14},{14,16},{16... | collective-permute-start | bytes 1572872 | tf_op jit(solution)/shard_map/ppermute | solution.py:22
  230.6 43.7 %copy-start.2 = (bf16[2,256,512]{2,1,0:T(8,128)(2,1)}, bf16[2,256,512]{2,1,0:T(8,128)(2,1)S(1)}, u32[]{:S(2)}) copy-start(bf16[2,256,512]{2,1,0:T(8,128)(2,1)S(1)} %collective-permute-done.1) | copy-start | bytes 1572868
  230.6 15.1 %collective-permute-start.2 = (bf16[2,256,512]{2,1,0:T(8,128)(2,1)S(1)}, bf16[2,256,512]{2,1,0:T(8,128)(2,1)S(1)}, u32[]{:S(2)}, u32[]{:S(2)}) collective-permute-start(bf16[2,256,512]{2,1,0:T(8,128)(2,1)S(1)} %collective-permute-done.1), channel_id=1, source_target_pairs={{126,0},{0,2},{2,4},{4,6},{6,8},{8,10},{10,12},{12,14},{14,16},{16... | collective-permute-start | bytes 1572872 | tf_op jit(solution)/shard_map/ppermute | solution.py:22
  245.7 0.8 copy-start.4
  246.5 14.3 %collective-permute-start.3 = (bf16[2,256,512]{2,1,0:T(8,128)(2,1)S(1)}, bf16[2,256,512]{2,1,0:T(8,128)(2,1)S(1)}, u32[]{:S(2)}, u32[]{:S(2)}) collective-permute-start(bf16[2,256,512]{2,1,0:T(8,128)(2,1)S(1)} %collective-permute-done.2), channel_id=1, source_target_pairs={{126,0},{0,2},{2,4},{4,6},{6,8},{8,10},{10,12},{12,14},{14,16},{16... | collective-permute-start | bytes 1572872 | tf_op jit(solution)/shard_map/ppermute | solution.py:22
  260.8 13.5 %copy-start.6 = (bf16[2,256,512]{2,1,0:T(8,128)(2,1)}, bf16[2,256,512]{2,1,0:T(8,128)(2,1)S(1)}, u32[]{:S(2)}) copy-start(bf16[2,256,512]{2,1,0:T(8,128)(2,1)S(1)} %collective-permute-done.3) | copy-start | bytes 1572868
  260.8 13.5 %collective-permute-start.4 = (bf16[2,256,512]{2,1,0:T(8,128)(2,1)S(1)}, bf16[2,256,512]{2,1,0:T(8,128)(2,1)}, u32[]{:S(2)}, u32[]{:S(2)}) collective-permute-start(bf16[2,256,512]{2,1,0:T(8,128)(2,1)S(1)} %collective-permute-done.3), channel_id=1, source_target_pairs={{126,0},{0,2},{2,4},{4,6},{6,8},{8,10},{10,12},{12,14},{14,16},{16... | collective-permute-start | bytes 1572872 | tf_op jit(solution)/shard_map/ppermute | solution.py:22
  274.3 12.9 %collective-permute-start.5 = (bf16[2,256,512]{2,1,0:T(8,128)(2,1)}, bf16[2,256,512]{2,1,0:T(8,128)(2,1)}, u32[]{:S(2)}, u32[]{:S(2)}) collective-permute-start(bf16[2,256,512]{2,1,0:T(8,128)(2,1)} %collective-permute-done.4), channel_id=1, source_target_pairs={{126,0},{0,2},{2,4},{4,6},{6,8},{8,10},{10,12},{12,14},{14,16},{16... | collective-permute-start | bytes 1572872 | tf_op jit(solution)/shard_map/ppermute | solution.py:22
  275.5 28.4 %copy-start.3 = (bf16[2,256,512]{2,1,0:T(8,128)(2,1)S(1)}, bf16[2,256,512]{2,1,0:T(8,128)(2,1)}, u32[]{:S(2)}) copy-start(bf16[2,256,512]{2,1,0:T(8,128)(2,1)} %copy-done.2) | copy-start | bytes 1572868
  287.1 12.4 %collective-permute-start.6 = (bf16[2,256,512]{2,1,0:T(8,128)(2,1)}, bf16[2,256,512]{2,1,0:T(8,128)(2,1)S(1)}, u32[]{:S(2)}, u32[]{:S(2)}) collective-permute-start(bf16[2,256,512]{2,1,0:T(8,128)(2,1)} %collective-permute-done.5), channel_id=1, source_target_pairs={{126,0},{0,2},{2,4},{4,6},{6,8},{8,10},{10,12},{12,14},{14,16},{16... | collective-permute-start | bytes 1572872 | tf_op jit(solution)/shard_map/ppermute | solution.py:22
  304.1 1.9 copy-start.7
  317.2 7.5 %copy-start.5 = (bf16[256,1024]{0,1:T(8,128)(2,1)S(1)}, bf16[256,1024]{0,1:T(8,128)(2,1)}, u32[]{:S(2)}) copy-start(bf16[256,1024]{0,1:T(8,128)(2,1)} %copy.83) | copy-start | bytes 1572868
  354.7 7.5 %copy-start.1 = (bf16[256,1024]{0,1:T(8,128)(2,1)S(1)}, bf16[256,1024]{0,1:T(8,128)(2,1)}, u32[]{:S(2)}) copy-start(bf16[256,1024]{0,1:T(8,128)(2,1)} %copy.81) | copy-start | bytes 1572868
Sparse Core Ops, SparseCore 0:
  9.2 38.2 all-gather.4
  50.0 137.6 all-gather.2
where the time goes:
time: 390 us; the launch traced here: 389 us
  waiting for transfers between devices  266 us (68%)
  matrix products  88.2 us (23%)
  between operations  14.4 us (4%)
  local copies, waits for them, and re-layouts  12.1 us (3%)
  other arithmetic  5.82 us (1%)
    all_gather x1, waiting for transfers between devices, side_by_side(): result = lax.all_gather(both, axis, axis=dim, tiled=True)  140 us
    ppermute x7, waiting for transfers between devices, shifted(): return lax.ppermute(block, axis, route)  87.7 us
    sub x4, matrix products, per_device(): weights = jnp.where(allowed[None], jnp.exp(masked - row_peak), 0.0)  44.9 us
    all_gather x1, waiting for transfers between devices, per_device(): full_tokens = lax.all_gather(tokens, 'mp', axis=1, tiled=True)  36.9 us
    dot_general x4, matrix products, per_device(): jnp.einsum('gtw,wd->tgd', probability, value_part, preferred_element_type...  29.1 us
    dot_general x2, matrix products, add_rows(): return jnp.dot(full_tokens, weight_rows, preferred_element_type=jnp.float32)  14.2 us
    unnamed x27, local copies, waits for them, and re-layouts  9.6 us
  transfers between devices with their start and end apart: 9, of which 9 were waited for; matrix products, arithmetic and copies ran while one was open for 2% of the time, Pallas kernels for 0%

commit v1 on v0

v1 whole, which is shorter than its diff:
```python
import functools
import math

import jax
import jax.numpy as jnp
from jax import lax
from jax.experimental import pallas as pl
from jax.experimental.pallas import tpu as pltpu
from jax.sharding import PartitionSpec as P

DH = 128
ROW = 2048
MESH = pl.DeviceIdType.MESH
PLUS, MINUS = 0, 1


def remote(src, dst, send, recv, device):
    return pltpu.make_async_remote_copy(
        src_ref=src,
        dst_ref=dst,
        send_sem=send,
        recv_sem=recv,
        device_id=device,
        device_id_type=MESH,
    )


def meet(neighbours):
    barrier = pltpu.get_barrier_semaphore()
    for device in neighbours:
        pl.semaphore_signal(barrier, inc=1, device_id=device, device_id_type=MESH)
    pl.semaphore_wait(barrier, len(neighbours))


def turned(x, table):
    half = DH // 2
    lane = lax.broadcasted_iota(jnp.int32, table.shape, 1)
    other = pltpu.roll(table, half, 1)
    cosine = jnp.where(lane < half, table, other)
    sine = jnp.where(lane < half, -other, table)
    return x * cosine + pltpu.roll(x, half, 1) * sine


def project_kernel(
    side, tokens, weight, table, kv, tok, w_all, tab, acc, give, got, local_sem,
    one_send, one_recv, two_send, two_recv, sib_send, sib_recv, z_send, z_recv,
):
    g, d, m = lax.axis_index("groups"), lax.axis_index("dp"), lax.axis_index("mp")
    x, y = lax.rem(d, side), lax.div(d, side)
    p = (1 - m) * x + m * y
    q = (1 - m) * y + m * x
    rows = weight.shape[0]
    count = tokens.shape[0]
    heads = kv.shape[0]
    per_half = side * side // 2
    z_parts = z_send.shape[0] - 3
    far = side // 2

    def wrap(i):
        return lax.rem(i + side, side)

    def spot(p_, q_):
        return (g, (1 - m) * (q_ * side + p_) + m * (p_ * side + q_), m)

    one_next = (spot(wrap(p + 1), q), spot(wrap(p - 1), q))
    two_next = (spot(p, wrap(q + 1)), spot(p, wrap(q - 1)))
    sibling = (g, d, 1 - m)
    partner = (g + 1 - 2 * lax.rem(g, 2), d, m)

    def block(c, k):
        return w_all.at[c, pl.ds(pl.multiple_of(k * rows, rows), rows)]

    def reach(r, way):
        return far if (r + way) % 2 == 0 else far - 1

    def one_copy(way, s, source=None):
        k = wrap(p - s) if way == PLUS else wrap(p + s)
        return remote(block(q, k), block(q, k), one_send.at[way, s - 1],
                      one_recv.at[way, s - 1], one_next[way])

    def one_start(way, s):
        k = wrap(p - s + 1) if way == PLUS else wrap(p + s - 1)
        source = weight if s == 1 else block(q, k)
        remote(source, block(q, k), one_send.at[way, s - 1],
               one_recv.at[way, s - 1], one_next[way]).start()

    def two_copy(r, way, s):
        c = wrap(q - s) if way == PLUS else wrap(q + s)
        k = wrap(p + r)
        return remote(block(c, k), block(c, k), two_send.at[r, way, s - 1],
                      two_recv.at[r, way, s - 1], two_next[way])

    def two_start(r, way, s):
        c = wrap(q - s + 1) if way == PLUS else wrap(q + s - 1)
        k = wrap(p + r)
        source = weight if (r == 0 and isinstance(s, int) and s == 1) else block(c, k)
        remote(source, block(c, k), two_send.at[r, way, s - 1],
               two_recv.at[r, way, s - 1], two_next[way]).start()

    def token_chunk(part, c):
        pieces = []
        for k in range(side):
            at = (1 - m) * (side * c + k) + m * (side * k + c)
            lanes = pl.ds(pl.multiple_of(lax.rem(at, per_half) * rows, rows), rows)
            pieces.append(tok[part, lax.div(at, per_half), :, lanes])
        return jnp.concatenate(pieces, axis=1)

    def add_chunk(c):
        acc[0] += jnp.dot(token_chunk(0, c), w_all[c], preferred_element_type=jnp.float32)

    z_rows = count // z_parts

    def z_part(i):
        return (pl.ds(i * z_rows, z_rows),)

    def z_tokens(i):
        at = pl.ds(i * z_rows, z_rows)
        return remote(tokens.at[at], tok.at[1, m, at], z_send.at[i], z_recv.at[i], partner)

    def pass_tokens(i):
        at = pl.ds(i * z_rows, z_rows)
        return remote(tok.at[1, m, at], tok.at[1, m, at], sib_send.at[1 + i],
                      sib_recv.at[1 + i], sibling)

    def sibling_tokens(i):
        at = pl.ds(i * z_rows, z_rows)
        return remote(tok.at[1, 1 - m, at], tok.at[1, 1 - m, at], sib_send.at[1 + i],
                      sib_recv.at[1 + i], sibling)

    own_weight = pltpu.make_async_copy(weight, block(q, p), local_sem.at[0])
    own_tokens = pltpu.make_async_copy(tokens, tok.at[0, m], local_sem.at[1])
    own_weight.start()
    own_tokens.start()
    meet(one_next + two_next + (sibling, partner))
    for way in (PLUS, MINUS):
        one_start(way, 1)
        two_start(0, way, 1)
    z_table = remote(table, tab, z_send.at[z_parts], z_recv.at[z_parts], partner)
    z_table.start()
    for i in range(z_parts):
        z_tokens(i).start()
    half_tokens = remote(tokens, tok.at[0, m], sib_send.at[0], sib_recv.at[0], sibling)
    half_tokens.start()
    acc[...] = jnp.zeros_like(acc)

    for s in range(1, far + 1):
        for way in (PLUS, MINUS):
            if s > (far if way == PLUS else far - 1):
                continue
            one_copy(way, s).wait_recv()
            if s < (far if way == PLUS else far - 1):
                one_start(way, s + 1)
            r = (-s) % side if way == PLUS else s
            for second in (PLUS, MINUS):
                two_start(r, second, 1)
    own_weight.wait()
    own_tokens.wait()
    remote(tok.at[0, 1 - m], tok.at[0, 1 - m], sib_send.at[0], sib_recv.at[0], sibling).wait_recv()

    order = [0]
    for s in range(1, far + 1):
        order += [(-s) % side] if s == far else [(-s) % side, s]

    def step(s, last):
        for r in order:
            for way in (PLUS, MINUS):
                if last:
                    if reach(r, way) == far:
                        two_copy(r, way, s).wait_recv()
                    continue
                two_copy(r, way, s).wait_recv()
                if reach(r, way) == far:
                    two_start(r, way, s + 1)
                else:
                    @pl.when(s < far - 1)
                    def _():
                        two_start(r, way, s + 1)

    add_chunk(q)

    @pl.loop(1, far)
    def _(s):
        step(s, False)
        z_tokens(s - 1).wait_recv()
        pass_tokens(s - 1).start()
        add_chunk(wrap(q - s))
        add_chunk(wrap(q + s))

    step(far, True)
    z_tokens(far - 1).wait_recv()
    pass_tokens(far - 1).start()
    for i in range(z_parts):
        sibling_tokens(i).wait_recv()
    z_table.wait_recv()

    even = lax.rem(g, 2) == 0
    plain = jnp.where(lax.broadcasted_iota(jnp.int32, tab.shape, 1) < DH // 2, 1.0, 0.0)
    span = acc.shape[2] // 2
    per_span = heads // 2

    def result(part, head, angles):
        return turned(acc[part, :, head * DH:(head + 1) * DH], angles).astype(jnp.bfloat16)

    def z_result(half):
        at = pl.ds(half * per_span, per_span)
        return remote(give.at[at], got.at[at], z_send.at[z_parts + 1 + half],
                      z_recv.at[z_parts + 1 + half], partner)

    theirs = jnp.where(even, tab[...], plain)
    for half in range(2):
        lanes = slice(half * span, (half + 1) * span)

        @pl.loop(0, side)
        def _(c):
            acc[1, :, lanes] += jnp.dot(
                token_chunk(1, c), w_all[c, :, lanes], preferred_element_type=jnp.float32
            )

        for head in range(half * per_span, (half + 1) * per_span):
            give[head] = result(1, head, theirs)
        z_result(half).start()
    add_chunk(wrap(q + far))
    ours = jnp.where(even, table[...], plain)
    mine = [result(0, head, ours) for head in range(heads)]
    for half in range(2):
        z_result(half).wait_recv()
        for head in range(half * per_span, (half + 1) * per_span):
            kv[head, :, :DH] = jnp.where(even, mine[head], got[head])
            kv[head, :, DH:] = jnp.where(even, got[head], mine[head])

    for way in (PLUS, MINUS):
        for s in range(1, far + 1 - way):
            one_copy(way, s).wait_send()
        for r in range(side):
            for s in range(1, reach(r, way) + 1):
                two_copy(r, way, s).wait_send()
    half_tokens.wait_send()
    z_table.wait_send()
    for i in range(z_parts):
        z_tokens(i).wait_send()
        pass_tokens(i).wait_send()
    for half in range(2):
        z_result(half).wait_send()


def attend_kernel(
    side, kv, queries, start, out, line, below, bias, local_sem,
    ring_send, ring_recv, up_send, up_recv,
):
    g, d, m = lax.axis_index("groups"), lax.axis_index("dp"), lax.axis_index("mp")
    x, y = lax.rem(d, side), lax.div(d, side)
    heads, count = kv.shape[0], kv.shape[1]
    group = queries.shape[1] // DH // heads
    far = side // 2
    half_row = far * count
    is_second = x < far

    def wrap(i):
        return lax.rem(i + side, side)

    ring = ((g, y * side + wrap(x + 1), m), (g, y * side + wrap(x - 1), m))
    above = (g, wrap(y + 1) * side + x, m)
    under = (g, wrap(y - 1) * side + x, m)

    def slot(h, at):
        return line.at[h, pl.ds(pl.multiple_of(at * count, count), count)]

    def up_slot(h, at):
        return below.at[h, pl.ds(pl.multiple_of(at * count, count), count)]

    def ring_copy(h, way, s):
        at = wrap(x - s) if way == PLUS else wrap(x + s)
        return remote(slot(h, at), slot(h, at), ring_send.at[h, way, s - 1],
                      ring_recv.at[h, way, s - 1], ring[way])

    def ring_start(h, way, s):
        at = wrap(x - s + 1) if way == PLUS else wrap(x + s - 1)
        remote(slot(h, at), slot(h, at), ring_send.at[h, way, s - 1],
               ring_recv.at[h, way, s - 1], ring[way]).start()

    def own_start(h):
        for way in (PLUS, MINUS):
            remote(kv.at[h], slot(h, x), ring_send.at[h, way, 0],
                   ring_recv.at[h, way, 0], ring[way]).start()

    def up_copy(h, at):
        return remote(slot(h, at + far), up_slot(h, at), up_send.at[h, at],
                      up_recv.at[h, at], above)

    def event(h, s):
        for way in (PLUS, MINUS):
            long_way = lax.rem(h + way, 2) == 0
            at = wrap(x - s) if way == PLUS else wrap(x + s)

            @pl.when((s < far) | long_way)
            def _():
                ring_copy(h, way, s).wait_recv()

                @pl.when((s < far - 1) | ((s == far - 1) & long_way))
                def _():
                    ring_start(h, way, s + 1)

                @pl.when(is_second & (at >= far))
                def _():
                    up_copy(h, at - far).start()

    own = [pltpu.make_async_copy(kv.at[h], slot(h, x), local_sem.at[h]) for h in range(heads)]
    for copy in own:
        copy.start()
    meet(ring + (above, under))
    own_start(0)
    own_start(1)

    @pl.when(jnp.logical_not(is_second))
    def _():
        below[...] = jnp.zeros_like(below)

    place = half_row + lax.rem(x, far) * count
    row = lax.broadcasted_iota(jnp.int32, (count, DH), 0) + place
    lane = lax.broadcasted_iota(jnp.int32, (count, DH), 1)
    for j in range(2 * half_row // DH):
        key = lane + j * DH
        fits = (key >= start[...]) & (key <= row)
        bias[:, j * DH:(j + 1) * DH] = jnp.where(fits, 0.0, -1e30)
    for copy in own:
        copy.wait()

    factor = math.log2(math.e) / math.sqrt(DH)
    base = pl.multiple_of((1 - lax.div(x + far, side)) * 0 + lax.div(x, far) * half_row, half_row)
    sub = 128
    contract = (((1,), (1,)), ((), ()))

    def piece(h, i):
        lanes = pl.ds(pl.multiple_of((h * group + i) * DH, DH), DH)
        for b in range(count // sub):
            at = slice(b * sub, (b + 1) * sub)
            q = queries[at, lanes]
            first = lax.dot_general(q, below[h, :, :DH], contract,
                                    preferred_element_type=jnp.float32) + bias[at, :half_row]
            second = lax.dot_general(q, line[h, pl.ds(base, half_row), :DH], contract,
                                     preferred_element_type=jnp.float32) + bias[at, half_row:]
            peak = jnp.maximum(jnp.max(first, axis=1, keepdims=True),
                               jnp.max(second, axis=1, keepdims=True))
            first = jnp.exp2((first - peak) * factor)
            second = jnp.exp2((second - peak) * factor)
            total = jnp.sum(first, axis=1, keepdims=True) + jnp.sum(second, axis=1, keepdims=True)
            scale = 1.0 / total
            mixed = jnp.dot((first * scale).astype(jnp.bfloat16), below[h, :, DH:],
                            preferred_element_type=jnp.float32)
            mixed += jnp.dot((second * scale).astype(jnp.bfloat16),
                             line[h, pl.ds(base, half_row), DH:],
                             preferred_element_type=jnp.float32)
            out[at, lanes] = mixed.astype(jnp.bfloat16)

    lag = far + 1
    units = group // 2

    @pl.loop(1, 2 * heads + lag)
    def _(k):
        h_one = lax.div(k - 1, 2)
        s_one = 1 + lax.rem(k - 1, 2)
        h_two, s_two = h_one - 1, s_one + 2

        @pl.when((s_one == 1) & (h_one >= 1) & (h_one + 1 < heads))
        def _():
            own_start(h_one + 1)

        @pl.when((h_two >= 0) & (h_two < heads))
        def _():
            event(h_two, s_two)

        @pl.when(h_one < heads)
        def _():
            event(h_one, s_one)

        @pl.when(k >= lag)
        def _():
            h = lax.div(k - lag, 2)

            @pl.when((lax.rem(k - lag, 2) == 0) & is_second)
            def _():
                for at in range(far):
                    up_copy(h, at).wait_recv()

            @pl.loop(0, units)
            def _(i):
                piece(h, lax.rem(k - lag, 2) * units + i)

    @pl.loop(0, heads)
    def _(h):
        for way in (PLUS, MINUS):
            for s in range(1, far):
                ring_copy(h, way, s).wait_send()

            @pl.when(lax.rem(h + way, 2) == 0)
            def _():
                ring_copy(h, way, far).wait_send()

        @pl.when(is_second)
        def _():
            for at in range(far):
                up_copy(h, at).wait_send()


def per_device(side, tokens, queries, w_key, w_value, lengths):
    count, wide = tokens.shape
    columns = w_key.shape[1]
    heads = columns // DH
    far = side // 2
    half_row = ROW // 2
    g, d = lax.axis_index("groups"), lax.axis_index("dp")

    all_tokens = count * side * side
    first_token = (d * count - half_row + all_tokens) % all_tokens
    row_index = first_token // ROW
    row_lengths = lax.dynamic_slice_in_dim(lengths, row_index, 1, 0)[0]
    finish = jnp.cumsum(row_lengths)
    offsets = first_token - row_index * ROW + jnp.arange(count, dtype=jnp.int32)
    before = finish[None, :] <= offsets[:, None]
    started = jnp.sum(jnp.where(before, row_lengths[None, :], 0), axis=1)
    positions = (offsets - started).astype(jnp.float32)
    frequency = jnp.power(
        500000.0, -2.0 * jnp.arange(DH // 2, dtype=jnp.float32) / DH
    )
    angles = positions[:, None] * frequency[None, :]
    table = jnp.concatenate([jnp.cos(angles), jnp.sin(angles)], axis=1)
    shift = jnp.where(d % side >= far, half_row, 0)
    start = jnp.broadcast_to((started + shift)[:, None], (count, DH))
    weight = jnp.where(g % 2 == 0, w_key, w_value)

    vmem = pl.BlockSpec(memory_space=pltpu.VMEM)
    hbm = pl.BlockSpec(memory_space=pl.ANY)
    dma = pltpu.SemaphoreType.DMA
    rows = weight.shape[0]
    z_parts = far
    kv = pl.pallas_call(
        functools.partial(project_kernel, side),
        out_shape=jax.ShapeDtypeStruct((heads, count, 2 * DH), jnp.bfloat16),
        in_specs=[hbm, hbm, vmem],
        out_specs=vmem,
        scratch_shapes=[
            pltpu.VMEM((2, 2, count, wide), jnp.bfloat16),
            pltpu.VMEM((side, side * rows, columns), jnp.bfloat16),
            pltpu.VMEM((count, DH), jnp.float32),
            pltpu.VMEM((2, count, columns), jnp.float32),
            pltpu.VMEM((heads, count, DH), jnp.bfloat16),
            pltpu.VMEM((heads, count, DH), jnp.bfloat16),
            dma((2,)),
            dma((2, far)),
            dma((2, far)),
            dma((side, 2, far)),
            dma((side, 2, far)),
            dma((1 + z_parts,)),
            dma((1 + z_parts,)),
            dma((z_parts + 3,)),
            dma((z_parts + 3,)),
        ],
        compiler_params=pltpu.CompilerParams(collective_id=0, has_side_effects=True),
        name="project",
    )(tokens, weight, table)
    return pl.pallas_call(
        functools.partial(attend_kernel, side),
        out_shape=jax.ShapeDtypeStruct(queries.shape, jnp.bfloat16),
        in_specs=[hbm, vmem, vmem],
        out_specs=vmem,
        scratch_shapes=[
            pltpu.VMEM((heads, side * count, 2 * DH), jnp.bfloat16),
            pltpu.VMEM((heads, far * count, 2 * DH), jnp.bfloat16),
            pltpu.VMEM((count, 2 * half_row), jnp.float32),
            dma((heads,)),
            dma((heads, 2, far)),
            dma((heads, 2, far)),
            dma((heads, far)),
            dma((heads, far)),
        ],
        compiler_params=pltpu.CompilerParams(collective_id=1, has_side_effects=True),
        name="attend",
    )(kv, queries, start)


def solution(mesh):
    side = math.isqrt(mesh.shape["dp"])
    return jax.shard_map(
        functools.partial(per_device, side),
        mesh=mesh,
        in_specs=(
            P(("groups", "dp"), "mp"),
            P(("groups", "dp"), "mp"),
            P("dp", "mp"),
            P("dp", "mp"),
            P("groups", None),
        ),
        out_specs=P(("groups", "dp"), "mp"),
        check_vma=False,
    )
```

time: 390 us -> 187 us (0.48)
  waiting for transfers between devices: 266 us -> 0 us
  Pallas kernels: 0 us -> 179 us
  matrix products: 88.2 us -> 0 us
  between operations: 14.4 us -> 0.03 us
  local copies, waits for them, and re-layouts: 12.1 us -> 4.65 us
    pallas_call x0 -> x2, Pallas kernels: none -> 179 us  [the longest x1 91.6 us: per_device(): pl.pallas_call(functools.partial(project_kernel, side), out_shape=jax.Sha...]
    all_gather x2 -> x0, waiting for transfers between devices: 177 us -> none  [the longest x1 140 us: side_by_side(): result = lax.all_gather(both, axis, axis=dim, tiled=True)]
    ppermute x7 -> x0, waiting for transfers between devices: 87.7 us -> none  [shifted(): return lax.ppermute(block, axis, route)]
    sub x4 -> x0, matrix products: 44.9 us -> none  [per_device(): weights = jnp.where(allowed[None], jnp.exp(masked - row_peak), 0.0)]
    dot_general x6 -> x0, matrix products: 43.3 us -> none  [the longest x4 29.1 us: per_device(): jnp.einsum('gtw,wd->tgd', probability, value_part, preferred_element_type...]
    unnamed x27 -> x1, local copies, waits for them, and re-layouts: 9.6 us -> 3.13 us
  transfers between devices with their start and end apart: 9 -> 0, of which waited for: 9 -> 0; matrix products, arithmetic and copies ran while one was open for 2% -> 0% of each run, Pallas kernels for 0% -> 0%
where the time goes in v1:
time: 187 us
  Pallas kernels  179 us (96%)
  local copies, waits for them, and re-layouts  4.65 us (2%)
  other arithmetic  3.12 us (2%)
    pallas_call x1, Pallas kernels, per_device(): pl.pallas_call(functools.partial(project_kernel, side), out_shape=jax.Sha...  91.6 us
    pallas_call x1, Pallas kernels, per_device(): pl.pallas_call(functools.partial(attend_kernel, side), out_shape=jax.Shap...  87.1 us

profile of v1, /device:TPU:514, one launch (start us, length us, event | category | flops | bytes accessed | tf_op | source)
XLA Modules:
  0.0 186.5 jit_solution(13614222289148862705)
XLA Ops:
  0.0 0.7 fusion.1
  0.7 0.1 copy.8
  0.8 0.1 reduce
  1.0 0.1 select_reduce_fusion
  1.1 0.7 broadcast_in_dim.27.start
  1.8 1.6 broadcast_select_fusion.weight
  3.4 0.5 multiply_cosine_fusion
  3.9 0.7 pad_maximum_fusion.table
  4.6 91.6 %project.1.kv = bf16[4,256,256]{2,1,0:T(8,128)(2,1)} custom-call(bf16[256,4096]{1,0:T(8,128)(2,1)} %tokens.1, bf16[128,512]{1,0:T(8,128)(2,1)} %broadcast_select_fusion.weight, f32[256,128]{1,0:T(8,128)} %pad_maximum_fusion.table), custom_call_target="tpu_custom_call" | custom-call | tf_op jit(solution)/shard_map/project/pallas_call | solution.py:436
  96.3 87.1 %attend.1 = bf16[256,4096]{1,0:T(8,128)(2,1)} custom-call(bf16[4,256,256]{2,1,0:T(8,128)(2,1)} %project.1.kv, bf16[256,4096]{1,0:T(8,128)(2,1)} %queries.1, s32[256,128]{1,0:T(8,128)} %broadcast_in_dim.27.start), custom_call_target="tpu_custom_call" | custom-call | tf_op jit(solution)/shard_map/attend/pallas_call | solution.py:461
  183.4 3.1 %copy.10 = bf16[256,4096]{1,0:T(8,128)(2,1)} copy(bf16[256,4096]{1,0:T(8,128)(2,1)} %attend.1) | data formatting | bytes 4194304
  (4 shorter events, 0.1 us)

commit v2 on v1

--- a/solution.py
+++ b/solution.py
@@ -244,9 +244,11 @@
 
 
 def attend_kernel(
-    side, kv, queries, start, out, line, below, bias, local_sem,
-    ring_send, ring_recv, up_send, up_recv,
+    side, kv, queries, start, out, line, below, bias, score_a, score_b, peak_a, peak_b,
+    weight_a, weight_b, total_a, total_b, local_sem, ring_send, ring_recv, up_send, up_recv,
 ):
+    scores, peaks = (score_a, score_b), (peak_a, peak_b)
+    weights, totals = (weight_a, weight_b), (total_a, total_b)
     g, d, m = lax.axis_index("groups"), lax.axis_index("dp"), lax.axis_index("mp")
     x, y = lax.rem(d, side), lax.div(d, side)
     heads, count = kv.shape[0], kv.shape[1]
@@ -327,30 +329,63 @@
 
     factor = math.log2(math.e) / math.sqrt(DH)
     base = pl.multiple_of((1 - lax.div(x + far, side)) * 0 + lax.div(x, far) * half_row, half_row)
-    sub = 128
     contract = (((1,), (1,)), ((), ()))
-
-    def piece(h, i):
-        lanes = pl.ds(pl.multiple_of((h * group + i) * DH, DH), DH)
-        for b in range(count // sub):
-            at = slice(b * sub, (b + 1) * sub)
-            q = queries[at, lanes]
-            first = lax.dot_general(q, below[h, :, :DH], contract,
-                                    preferred_element_type=jnp.float32) + bias[at, :half_row]
-            second = lax.dot_general(q, line[h, pl.ds(base, half_row), :DH], contract,
-                                     preferred_element_type=jnp.float32) + bias[at, half_row:]
-            peak = jnp.maximum(jnp.max(first, axis=1, keepdims=True),
-                               jnp.max(second, axis=1, keepdims=True))
-            first = jnp.exp2((first - peak) * factor)
-            second = jnp.exp2((second - peak) * factor)
-            total = jnp.sum(first, axis=1, keepdims=True) + jnp.sum(second, axis=1, keepdims=True)
-            scale = 1.0 / total
-            mixed = jnp.dot((first * scale).astype(jnp.bfloat16), below[h, :, DH:],
-                            preferred_element_type=jnp.float32)
-            mixed += jnp.dot((second * scale).astype(jnp.bfloat16),
-                             line[h, pl.ds(base, half_row), DH:],
-                             preferred_element_type=jnp.float32)
-            out[at, lanes] = mixed.astype(jnp.bfloat16)
+    keys = 2 * half_row
+    wide, tall = 512, 64
+
+    def key_rows(j):
+        if j < half_row:
+            return below, pl.ds(j, wide)
+        return line, pl.ds(pl.multiple_of(base + j - half_row, wide), wide)
+
+    def lanes_of(t):
+        return pl.ds(pl.multiple_of(t * DH, DH), DH)
+
+    def score(t, into):
+        h = lax.div(t, group)
+        q = queries[:, lanes_of(t)]
+        peak = None
+        for j in range(0, keys, wide):
+            ref, rows = key_rows(j)
+            s = lax.dot_general(q, ref[h, rows, :DH], contract,
+                                preferred_element_type=jnp.float32) + bias[:, j:j + wide]
+            scores[into][:, j:j + wide] = s
+            for b in range(0, wide, DH):
+                part = s[:, b:b + DH]
+                peak = part if peak is None else jnp.maximum(peak, part)
+        peaks[into][...] = peak
+
+    def weigh(into):
+        for r in range(0, count, tall):
+            at = slice(r, r + tall)
+            peak = jnp.max(peaks[into][at], axis=1, keepdims=True)
+            total = jnp.zeros((tall, DH), jnp.float32)
+            for j in range(0, keys, 2 * DH):
+                e = jnp.exp2((scores[into][at, j:j + 2 * DH] - peak) * factor)
+                total += e[:, :DH] + e[:, DH:]
+                weights[into][at, j:j + 2 * DH] = e.astype(jnp.bfloat16)
+            totals[into][at] = total
+
+    def mix(t, into):
+        h = lax.div(t, group)
+        mixed = None
+        for j in range(0, keys, half_row):
+            ref = below if j < half_row else line
+            rows = pl.ds(0, half_row) if j < half_row else pl.ds(base, half_row)
+            part = jnp.dot(weights[into][:, j:j + half_row], ref[h, rows, DH:],
+                           preferred_element_type=jnp.float32)
+            mixed = part if mixed is None else mixed + part
+        total = jnp.sum(totals[into][...], axis=1, keepdims=True)
+        out[:, lanes_of(t)] = (mixed / total).astype(jnp.bfloat16)
+
+    def pair(t):
+        last = lax.rem(t, group) == group - 2
+        score(t + 1, 1)
+        weigh(0)
+        mix(jnp.maximum(t - 1, 0), 1)
+        score(jnp.where(last, t, t + 2), 0)
+        weigh(1)
+        mix(t, 0)
 
     lag = far + 1
     units = group // 2
@@ -382,9 +417,15 @@
                 for at in range(far):
                     up_copy(h, at).wait_recv()
 
-            @pl.loop(0, units)
+            @pl.when(lax.rem(k - lag, 2) == 0)
+            def _():
+                score(h * group, 0)
+
+            @pl.loop(0, units // 2)
             def _(i):
-                piece(h, lax.rem(k - lag, 2) * units + i)
+                pair((k - lag) * units + 2 * i)
+
+    mix(heads * group - 1, 1)
 
     @pl.loop(0, heads)
     def _(h):
@@ -467,6 +508,14 @@
             pltpu.VMEM((heads, side * count, 2 * DH), jnp.bfloat16),
             pltpu.VMEM((heads, far * count, 2 * DH), jnp.bfloat16),
             pltpu.VMEM((count, 2 * half_row), jnp.float32),
+            pltpu.VMEM((count, 2 * half_row), jnp.float32),
+            pltpu.VMEM((count, 2 * half_row), jnp.float32),
+            pltpu.VMEM((count, DH), jnp.float32),
+            pltpu.VMEM((count, DH), jnp.float32),
+            pltpu.VMEM((count, 2 * half_row), jnp.bfloat16),
+            pltpu.VMEM((count, 2 * half_row), jnp.bfloat16),
+            pltpu.VMEM((count, DH), jnp.float32),
+            pltpu.VMEM((count, DH), jnp.float32),
             dma((heads,)),
             dma((heads, 2, far)),
             dma((heads, 2, far)),

time: 187 us -> 176 us (0.941)
  Pallas kernels: 179 us -> 168 us
    pallas_call x1, Pallas kernels: 87.1 us -> 76.3 us  [per_device(): pl.pallas_call(functools.partial(attend_kernel, side), out_shape=jax.Shap...]
where the time goes in v2:
time: 176 us
  Pallas kernels  168 us (95%)
  local copies, waits for them, and re-layouts  4.65 us (3%)
  other arithmetic  3.12 us (2%)
    pallas_call x1, Pallas kernels, per_device(): pl.pallas_call(functools.partial(project_kernel, side), out_shape=jax.Sha...  91.6 us
    pallas_call x1, Pallas kernels, per_device(): pl.pallas_call(functools.partial(attend_kernel, side), out_shape=jax.Shap...  76.3 us

profile of v2, /device:TPU:514, one launch (start us, length us, event | category | flops | bytes accessed | tf_op | source)
XLA Modules:
  0.0 175.7 jit_solution(12929179962862542142)
XLA Ops:
  0.0 0.7 fusion.1
  0.7 0.1 copy.8
  0.8 0.1 reduce
  1.0 0.1 select_reduce_fusion
  1.1 0.7 broadcast_in_dim.27.start
  1.8 1.6 broadcast_select_fusion.weight
  3.4 0.5 multiply_cosine_fusion
  3.9 0.7 pad_maximum_fusion.table
  4.6 91.6 %project.1.kv = bf16[4,256,256]{2,1,0:T(8,128)(2,1)} custom-call(bf16[256,4096]{1,0:T(8,128)(2,1)} %tokens.1, bf16[128,512]{1,0:T(8,128)(2,1)} %broadcast_select_fusion.weight, f32[256,128]{1,0:T(8,128)} %pad_maximum_fusion.table), custom_call_target="tpu_custom_call" | custom-call | tf_op jit(solution)/shard_map/project/pallas_call | solution.py:477
  96.3 76.3 %attend.1 = bf16[256,4096]{1,0:T(8,128)(2,1)} custom-call(bf16[4,256,256]{2,1,0:T(8,128)(2,1)} %project.1.kv, bf16[256,4096]{1,0:T(8,128)(2,1)} %queries.1, s32[256,128]{1,0:T(8,128)} %broadcast_in_dim.27.start), custom_call_target="tpu_custom_call" | custom-call | tf_op jit(solution)/shard_map/attend/pallas_call | solution.py:502
  172.6 3.1 %copy.10 = bf16[256,4096]{1,0:T(8,128)(2,1)} copy(bf16[256,4096]{1,0:T(8,128)(2,1)} %attend.1) | data formatting | bytes 4194304
  (4 shorter events, 0.1 us)
